TPU v7x, 32 devices: a whole 2x2x4 slice. The times are simulated.
32 devices in a mesh: row: 4 (over x, core), col: 8 (over z, y).
Axes of the slice: x: 2, y: 2, z: 4, core: 2. Of those that a mesh axis runs over, the one named last changes fastest.
Arguments:
- tile_weight: bfloat16 [32, 32, 2, 128, 128], P(('row', 'col')), may hold values from 0.049804688 to 1
- tile_angle: bfloat16 [32, 32, 2, 128, 128], P(('row', 'col')), may hold values from -3.140625 to 3.140625
- tile_list: int32 [32, 32, 2, 2], P(('row', 'col')), may hold values from 0 to 63, as said below
- tile_count: int32 [32, 32], P(('row', 'col')), may hold values from 0 to 2, as said below
- init_basis: float32 [2, 32, 8192], P(None, None, ('row', 'col')), may hold values from -6 to 6
Outputs:
- basis: float32 [2, 32, 8192], P(None, None, ('row', 'col'))
Inputs may be any that keep to these rules, and one draw needn't show every extreme that they name: `tile_list`: let piece(b) = b // 2 for a block b, and number devices s = a * 8 + e' along row+col. For device s = a * 8 + b' and destination d = f * 8 + e, slot [s, d, k] holds I with piece(I) = a * 8 + e and J with piece(J) = f * 8 + b'. The slots of one s, d hold distinct tiles; for d = s they hold the diagonal tiles (I, I) of the first 2 blocks of the device's piece. tile_count[s, s] = 2, and one destination has 2 live slots from every device.
All inputs are finite; a program needn't handle non-finite values.
Results may differ from a plain program's by a relative error of at most 0.0053.
Values may be sent and summed in bfloat16 or wider, within the bound.
A program may use at most 256 MiB of HBM per device.

v0:
```python
import jax
import jax.numpy as jnp
from jax import lax
from jax.sharding import PartitionSpec as P

ITERS = 3


def complex_tiles(weight, angle):
    weight_f = weight.astype(jnp.float32)
    angle_f = angle.astype(jnp.float32)
    return (
        (weight_f * jnp.cos(angle_f)).astype(jnp.bfloat16),
        (weight_f * jnp.sin(angle_f)).astype(jnp.bfloat16),
    )


def highest_dot(left, right):
    return jnp.dot(left, right, precision=lax.Precision.HIGHEST, preferred_element_type=jnp.float32)


def gram_terms(image_real, image_imag):
    gram_real = highest_dot(image_real, image_real.T) + highest_dot(image_imag, image_imag.T)
    gram_imag = highest_dot(image_real, image_imag.T) - highest_dot(image_imag, image_real.T)
    return (gram_real, gram_imag)


def orthonormal(gram_real, gram_imag, image_real, image_imag):
    width = gram_real.shape[0]
    indices = jnp.arange(width)
    ridge = 0.01 * jnp.trace(gram_real) / width + 1e-06
    gram_real = gram_real + ridge * jnp.eye(width, dtype=jnp.float32)
    lower_real = jnp.zeros((width, width), jnp.float32)
    lower_imag = jnp.zeros((width, width), jnp.float32)
    for column in range(width):
        prod_real = highest_dot(lower_real, lower_real[column]) + highest_dot(
            lower_imag, lower_imag[column]
        )
        prod_imag = highest_dot(lower_imag, lower_real[column]) - highest_dot(
            lower_real, lower_imag[column]
        )
        pivot = jnp.sqrt(gram_real[column, column] - prod_real[column])
        below = indices > column
        col_real = (gram_real[:, column] - prod_real) / pivot
        col_imag = (gram_imag[:, column] - prod_imag) / pivot
        lower_real = lower_real.at[:, column].set(
            jnp.where(below, col_real, jnp.where(indices == column, pivot, 0.0))
        )
        lower_imag = lower_imag.at[:, column].set(jnp.where(below, col_imag, 0.0))
    inv_real = jnp.zeros((width, width), jnp.float32)
    inv_imag = jnp.zeros((width, width), jnp.float32)
    for column in range(width):
        unit = (indices == column).astype(jnp.float32)
        sum_real = highest_dot(lower_real[column], inv_real) - highest_dot(
            lower_imag[column], inv_imag
        )
        sum_imag = highest_dot(lower_real[column], inv_imag) + highest_dot(
            lower_imag[column], inv_real
        )
        diag_value = lower_real[column, column]
        inv_real = inv_real.at[column].set((unit - sum_real) / diag_value)
        inv_imag = inv_imag.at[column].set(-sum_imag / diag_value)
    new_real = highest_dot(inv_real, image_real) + highest_dot(inv_imag, image_imag)
    new_imag = highest_dot(inv_real, image_imag) - highest_dot(inv_imag, image_real)
    return jnp.stack([new_real, new_imag], 0)


def one_hot(position, count, values):
    return (position[:, None] == jnp.arange(count)[None, :]).astype(jnp.float32) * values[:, None]


def place_rows(hot_table, sums):
    return jnp.einsum("ng,ni->gi", hot_table, sums, precision=lax.Precision.HIGHEST)


def to_blocks(gathered, tile):
    parts, width, length = gathered.shape
    return jnp.transpose(gathered.reshape(parts, width, length // tile, tile), (2, 0, 1, 3))


def forward_terms(real_part, imag_part, taken, hot_table):
    first = jnp.einsum("nskj,nij->nski", taken, real_part, preferred_element_type=jnp.float32)
    second = jnp.einsum("nskj,nij->nski", taken, imag_part, preferred_element_type=jnp.float32)
    terms = jnp.stack([first[:, 0] - second[:, 1], first[:, 1] + second[:, 0]], 1)
    return jnp.einsum("ng,nski->skgi", hot_table, terms, precision=lax.Precision.HIGHEST)


def mirror_terms(real_part, imag_part, taken, hot_table):
    first = jnp.einsum("chqr,crg->chqg", taken, real_part, preferred_element_type=jnp.float32)
    second = jnp.einsum("chqr,crg->chqg", taken, imag_part, preferred_element_type=jnp.float32)
    terms = jnp.stack([first[:, 0] + second[:, 1], first[:, 1] - second[:, 0]], 1)
    return jnp.einsum("ng,nski->skgi", hot_table, terms, precision=lax.Precision.HIGHEST)


def shards(tile_weight, tile_angle, tile_list, tile_count, init_basis):
    rows_axis = lax.axis_size("row")
    cols_axis = lax.axis_size("col")
    row_place = lax.axis_index("row")
    devices = rows_axis * cols_axis
    tile = tile_weight.shape[-1]
    pair_cap = tile_weight.shape[2]
    width = init_basis.shape[2]
    columns = init_basis.shape[1]
    per_device = width // tile
    group_rows = cols_axis * per_device
    slot_count = devices * pair_cap
    images_all = width * devices
    weights = tile_weight.reshape(slot_count, tile, tile)
    angles = tile_angle.reshape(slot_count, tile, tile)
    listing = tile_list.reshape(slot_count, 2)
    row_global = listing[:, 0]
    col_global = listing[:, 1]
    alive = (jnp.arange(pair_cap)[None, :] < tile_count.reshape(devices, 1)).reshape(slot_count)
    halves = jnp.where(alive, 0.5, 0.0).astype(jnp.float32)
    row_local = row_global - row_place * group_rows
    col_local = col_global // per_device // cols_axis * per_device + col_global % per_device
    real_part, imag_part = complex_tiles(weights, angles)
    row_hot = one_hot(row_local, group_rows, halves)
    degree_part = place_rows(row_hot, jnp.sum(weights, axis=2, dtype=jnp.float32))
    mirror_col = row_global // per_device // cols_axis * per_device + row_global % per_device
    mirror_row = col_global // per_device % cols_axis * per_device + col_global % per_device
    index_pairs = jnp.where(alive[:, None], jnp.stack([mirror_col, mirror_row], -1), -1)
    index_pairs = index_pairs.reshape(devices, pair_cap, 2)
    sent_weight, sent_angle = (
        lax.all_to_all(
            tile_weight.reshape(devices, pair_cap, tile, tile),
            ("row", "col"),
            split_axis=0,
            concat_axis=0,
            tiled=True,
        ),
        lax.all_to_all(
            tile_angle.reshape(devices, pair_cap, tile, tile),
            ("row", "col"),
            split_axis=0,
            concat_axis=0,
            tiled=True,
        ),
    )
    sent_index = lax.all_to_all(
        index_pairs, ("row", "col"), split_axis=0, concat_axis=0, tiled=True
    )
    recv_weight = sent_weight.reshape(slot_count, tile, tile)
    recv_angle = sent_angle.reshape(slot_count, tile, tile)
    recv_index = sent_index.reshape(slot_count, 2)
    recv_halves = jnp.where(recv_index[:, 0] >= 0, 0.5, 0.0).astype(jnp.float32)
    recv_take = jnp.maximum(recv_index[:, 0], 0)
    recv_put = jnp.maximum(recv_index[:, 1], 0)
    recv_real, recv_imag = complex_tiles(recv_weight, recv_angle)
    recv_hot = one_hot(recv_put, group_rows, recv_halves)
    degree_part = degree_part + place_rows(
        recv_hot, jnp.sum(recv_weight, axis=1, dtype=jnp.float32)
    )
    degree = lax.psum_scatter(
        degree_part.reshape(group_rows * tile), "col", scatter_dimension=0, tiled=True
    )
    scale = lax.rsqrt(degree)
    basis = init_basis
    for rounds in range(ITERS):
        scaled = (basis * scale).astype(jnp.bfloat16)
        col_blocks = to_blocks(lax.all_gather(scaled, "row", axis=2, tiled=True), tile)
        partial_value = forward_terms(real_part, imag_part, col_blocks[col_local], row_hot)
        partial_value = partial_value + mirror_terms(
            recv_real, recv_imag, col_blocks[recv_take], recv_hot
        )
        image = lax.psum_scatter(
            partial_value.reshape(2, columns, group_rows * tile),
            "col",
            scatter_dimension=2,
            tiled=True,
        )
        image = image * scale
        gram_real, gram_imag = gram_terms(image[0], image[1])
        gram_real, gram_imag = lax.psum((gram_real, gram_imag), ("row", "col"))
        basis = orthonormal(gram_real / images_all, gram_imag / images_all, image[0], image[1])
    return basis


def solution(mesh):
    placed = (
        P(("row", "col"), None, None, None, None),
        P(("row", "col"), None, None, None, None),
        P(("row", "col"), None, None, None),
        P(("row", "col"), None),
        P(None, None, ("row", "col")),
    )
    return jax.shard_map(
        shards, mesh=mesh, in_specs=placed, out_specs=P(None, None, ("row", "col")), check_vma=False
    )
```

profile of v0, /device:TPU:0, one launch (start us, length us, event | category | flops | bytes accessed | tf_op | source)
XLA Modules:
  0.0 1150.6 jit_solution(1223712497820123222)
XLA Ops:
  8.8 14.3 %all_to_all.15 = s32[32,2,2]{1,2,0:T(2,128)S(1)} all-to-all(s32[32,2,2]{1,2,0:T(2,128)S(1)} %copy.43), channel_id=1, replica_groups=mesh['row'=4,'col'=8] {'row','col'}, dimensions={0} | all-to-all | bytes 1024 | tf_op jit(solution)/shard_map/all_to_all | solution.py:140
  23.1 53.4 %all_to_all.16 = bf16[32,2,128,128]{3,2,1,0:T(8,128)(2,1)} all-to-all(bf16[32,2,128,128]{3,2,1,0:T(8,128)(2,1)} %bitcast.8317), channel_id=1, replica_groups=mesh['row'=4,'col'=8] {'row','col'}, dimensions={0} | all-to-all | bytes 4194304 | tf_op jit(solution)/shard_map/all_to_all | solution.py:132
  76.5 3.6 all-to-all-start.1
  81.7 17.8 %fusion = (bf16[1,32,2,128,128]{4,3,2,1,0:T(8,128)(2,1)S(1)}, bf16[1,32,2,128,128]{4,3,2,1,0:T(8,128)(2,1)}, f32[32,2,128]{2,1,0:T(2,128)S(1)}) fusion(bf16[1,32,2,128,128]{4,3,2,1,0:T(8,128)(2,1)} %param.774, bf16[1,32,2,128,128]{4,3,2,1,0:T(8,128)(2,1)} %param.773), kind=kLoop, calls=%fused_computation.16 | loop fusion | flops 7331840 | bytes 8421376 | tf_op jit(solution)/shard_map/convert_element_type | solution.py:13
  99.8 30.4 %all-to-all-done.1 = bf16[32,2,128,128]{3,2,1,0:T(8,128)(2,1)} async-done(((bf16[32,2,128,128]{3,2,1,0:T(8,128)(2,1)}), bf16[32,2,128,128]{3,2,1,0:T(8,128)(2,1)}, u32[]{:S(2)}, u32[]{:S(2)}) %all-to-all-start.1) | async-done | bytes 2097184 | tf_op jit(solution)/shard_map/all_to_all | solution.py:125
  130.2 17.7 %fusion.2 = (bf16[32,2,128,128]{3,2,1,0:T(8,128)(2,1)}, bf16[32,2,128,128]{3,2,1,0:T(8,128)(2,1)}, f32[32,2,128]{2,1,0:T(2,128)S(1)}) fusion(bf16[32,2,128,128]{3,2,1,0:T(8,128)(2,1)} %all_to_all.16, bf16[32,2,128,128]{3,2,1,0:T(8,128)(2,1)} %all-to-all-done.1), kind=kLoop, calls=%fused_computation.18 | loop fusion | flops 7331840 | bytes 8421376 | tf_op jit(solution)/shard_map/convert_element_type | solution.py:13
  148.1 17.8 %all-reduce.12 = f32[2048]{0:T(1024)S(1)} all-reduce(f32[2048]{0:T(1024)S(1)} %fusion.40), channel_id=2, replica_groups=mesh['row'=4,'col'=8] {'col'}, use_global_device_ids=true, to_apply=%region_3.4.clone | all-reduce | flops 2048 | bytes 16384
  166.0 5.6 all_gather.9
  172.4 2.4 fusion.2345
  176.2 3.2 fusion.12
  180.1 3.1 fusion.2343
  183.2 1.5 fusion.2342
  185.5 0.8 copy-done.7
  186.3 2.4 fusion.19
  188.7 0.9 reshape.9340
  210.3 39.9 %reduce-scatter.4.cloned.1.call-done = f32[2,32,256]{2,1,0:T(8,128)} async-done(((f32[2,32,2048]{2,1,0:T(8,128)}), f32[2,32,256]{2,1,0:T(8,128)}) %reduce-scatter.4.cloned.1.call-update) | async-done | bytes 65552 | tf_op jit(solution)/shard_map/reduce_scatter | solution.py:166
  250.2 0.8 broadcast_multiply_fusion.2
  251.7 40.8 %all-reduce.15 = (f32[32,32]{1,0:T(8,128)S(1)}, f32[32,32]{1,0:T(8,128)S(1)}) all-reduce(f32[32,32]{1,0:T(8,128)S(1)} %convolution_add_fusion.5, f32[32,32]{1,0:T(8,128)S(1)} %convolution_subtract_fusion.5), channel_id=1, replica_groups=mesh['row'=4,'col'=8] {'row','col'}, use_global_device_ids=true, to_apply=%region_5.6 | all-reduce | flops 2048 | bytes 16384 | tf_op jit(solution)/shard_map/psum | solution.py:174
  439.7 0.8 fusion.658
  440.5 0.8 fusion.660
  451.6 0.8 fusion.688
  452.5 0.8 fusion.690
  463.0 0.8 fusion.718
  463.9 0.8 fusion.720
  465.0 0.8 fusion.725
  465.8 0.8 fusion.723
  490.1 5.8 all_gather.10
  496.7 3.8 fusion.2349
  500.5 2.1 fusion.2348
  503.3 3.1 fusion.2347
  506.5 1.5 fusion.2346
  509.4 2.4 fusion.8
  512.4 2.4 fusion.25
  514.8 0.9 reshape.9470
  515.8 61.8 %reduce-scatter.6.cloned.1.call-done = f32[2,32,256]{2,1,0:T(8,128)} async-done(((f32[2,32,2048]{2,1,0:T(8,128)}), f32[2,32,256]{2,1,0:T(8,128)}) %reduce-scatter.6.cloned.1.call-update) | async-done | bytes 65552 | tf_op jit(solution)/shard_map/reduce_scatter | solution.py:166
  577.5 0.8 broadcast_multiply_fusion.1
  579.0 40.2 %all-reduce.14 = (f32[32,32]{1,0:T(8,128)S(1)}, f32[32,32]{1,0:T(8,128)S(1)}) all-reduce(f32[32,32]{1,0:T(8,128)S(1)} %convolution_add_fusion.4, f32[32,32]{1,0:T(8,128)S(1)} %convolution_subtract_fusion.4), channel_id=1, replica_groups=mesh['row'=4,'col'=8] {'row','col'}, use_global_device_ids=true, to_apply=%region_39.40 | all-reduce | flops 2048 | bytes 16384 | tf_op jit(solution)/shard_map/psum | solution.py:174
  767.0 0.8 fusion.938
  767.8 0.8 fusion.940
  778.9 0.8 fusion.968
  790.3 0.8 fusion.998
  791.2 0.8 fusion.1000
  792.3 0.8 fusion.1005
  793.1 0.8 fusion.1003
  817.4 6.0 all_gather.11
  824.2 3.8 fusion.2353
  827.9 2.0 fusion.2352
  830.7 3.1 fusion.2351
  833.8 1.5 fusion.2350
  836.7 2.4 fusion.4
  839.7 2.4 fusion.31
  842.1 0.9 reshape.9600
  843.0 61.3 %reduce-scatter.8.cloned.1.call-done = f32[2,32,256]{2,1,0:T(8,128)} async-done(((f32[2,32,2048]{2,1,0:T(8,128)}), f32[2,32,256]{2,1,0:T(8,128)}) %reduce-scatter.8.cloned.1.call-update) | async-done | bytes 65552 | tf_op jit(solution)/shard_map/reduce_scatter | solution.py:166
  904.3 0.8 broadcast_multiply_fusion
  905.9 40.4 %all-reduce.13 = (f32[32,32]{1,0:T(8,128)S(1)}, f32[32,32]{1,0:T(8,128)S(1)}) all-reduce(f32[32,32]{1,0:T(8,128)S(1)} %convolution_add_fusion.3, f32[32,32]{1,0:T(8,128)S(1)} %convolution_subtract_fusion.3), channel_id=1, replica_groups=mesh['row'=4,'col'=8] {'row','col'}, use_global_device_ids=true, to_apply=%region_43.44 | all-reduce | flops 2048 | bytes 16384 | tf_op jit(solution)/shard_map/psum | solution.py:174
  1086.4 0.8 fusion.1205
  1087.2 0.8 fusion.1203
  1098.1 0.8 fusion.1235
  1098.9 0.8 fusion.1233
  1100.1 0.8 fusion.1238
  1129.1 0.8 fusion.1315
  1129.9 0.8 fusion.1313
  1136.4 0.8 fusion.1335
  1137.3 0.8 fusion.1333
  (1665 shorter events, 482.3 us)
Async XLA Ops:
  76.5 3.7 copy-start.9
  76.5 3.9 copy-start.10
  76.5 53.7 %all-to-all-start.1 = ((bf16[32,2,128,128]{3,2,1,0:T(8,128)(2,1)}), bf16[32,2,128,128]{3,2,1,0:T(8,128)(2,1)}, u32[]{:S(2)}, u32[]{:S(2)}) async-start(bf16[32,2,128,128]{3,2,1,0:T(8,128)(2,1)} %bitcast.5), calls=%async_computation.1 | async-start | bytes 4194304 | tf_op jit(solution)/shard_map/all_to_all | solution.py:125
  80.2 170.0 %reduce-scatter.4.cloned.1.call-start = ((), (), s32[]{:S(2)}) async-start(), calls=%async_computation.6 | async-start | bytes 589824 | tf_op jit(solution)/shard_map/reduce_scatter | solution.py:166
  99.8 66.1 %copy-start.8 = (f32[2,32,256]{2,1,0:T(8,128)S(1)}, f32[2,32,256]{2,1,0:T(8,128)}, u32[]{:S(2)}) copy-start(f32[2,32,256]{2,1,0:T(8,128)} %param.777) | copy-start | bytes 196612
  172.4 2.4 copy-start
  185.2 1.0 copy-start.7
  189.6 388.0 %reduce-scatter.6.cloned.1.call-start = ((), (), s32[]{:S(2)}) async-start(), calls=%async_computation.7 | async-start | bytes 589824 | tf_op jit(solution)/shard_map/reduce_scatter | solution.py:166
  496.7 3.8 copy-start.1
  506.4 1.6 copy-start.5
  506.4 2.2 copy-start.6
  515.7 388.6 %reduce-scatter.8.cloned.1.call-start = ((), (), s32[]{:S(2)}) async-start(), calls=%async_computation.8 | async-start | bytes 589824 | tf_op jit(solution)/shard_map/reduce_scatter | solution.py:166
  824.2 3.8 copy-start.2
  833.8 1.6 copy-start.3
  833.8 2.2 copy-start.4
Sparse Core Ops, SparseCore 0:
  189.7 60.4 reduce-scatter.3
  515.8 61.6 reduce-scatter.5
  843.1 61.1 reduce-scatter.7
where the time goes:
time: 1160 us; the launch traced here: 1150 us
  matrix products  323 us (28%)
  blocking collectives  224 us (19%)
  waiting for transfers between devices  193 us (17%)
  between operations  142 us (12%)
  local copies, waits for them, and re-layouts  139 us (12%)
  other arithmetic  124 us (11%)
    dot_general x775, matrix products, highest_dot(): jnp.dot(left, right, precision=lax.Precision.HIGHEST, preferred_element_t...  279 us
    reduce_scatter x3, waiting for transfers between devices, shards(): lax.psum_scatter(partial_value.reshape(2, columns, group_rows * tile), 'c...  163 us
    psum x3, blocking collectives, shards(): gram_real, gram_imag = lax.psum((gram_real, gram_imag), ('row', 'col'))  121 us
    another operation x124, other arithmetic  78.8 us
    slice x99, local copies, waits for them, and re-layouts, orthonormal(): pivot = jnp.sqrt(gram_real[column, column] - prod_real[column])  63.6 us
    all_to_all x1, blocking collectives, shards(): lax.all_to_all(tile_angle.reshape(devices, pair_cap, tile, tile), ('row',...  53.4 us
    convert_element_type x2, other arithmetic, complex_tiles(): (weight_f * jnp.cos(angle_f)).astype(jnp.bfloat16)  35.6 us
    all_to_all x1, waiting for transfers between devices, shards(): lax.all_to_all(tile_weight.reshape(devices, pair_cap, tile, tile), ('row'...  30.4 us
  transfers between devices with their start and end apart: 4, of which 4 were waited for; matrix products, arithmetic and copies ran while one was open for 3% of the time, Pallas kernels for 0%

commit v1 on v0

v1 whole, which is shorter than its diff:
```python
import functools
import jax
import jax.numpy as jnp
from jax import lax
from jax.experimental import pallas as pl
from jax.experimental.pallas import tpu as pltpu
from jax.sharding import PartitionSpec as P

ITERS = 3
PART_DTYPE = jnp.bfloat16
MESH = pl.DeviceIdType.MESH
HIGH = lax.Precision.HIGHEST
NT = (((1,), (1,)), ((), ()))
NN = (((1,), (0,)), ((), ()))

SIN_TERMS = (-1.0 / 39916800, 1.0 / 362880, -1.0 / 5040, 1.0 / 120, -1.0 / 6, 1.0)
COS_TERMS = (1.0 / 479001600, -1.0 / 3628800, 1.0 / 40320, -1.0 / 720, 1.0 / 24, -0.5, 1.0)


def horner(terms, x):
    total = jnp.full_like(x, terms[0])
    for term in terms[1:]:
        total = total * x + term
    return total


def dot(left, right, dims, precision=None):
    return lax.dot_general(left, right, dims, precision=precision, preferred_element_type=jnp.float32)


def prep_kernel(cols, cap, per, tile, list_ref, count_ref, weight_ref, angle_ref, real_ref, imag_ref, rdeg_ref, cdeg_ref, held):
    f = pl.program_id(0)
    piece = per * tile

    @pl.when(f == 0)
    def _():
        rdeg_ref[...] = jnp.zeros_like(rdeg_ref)

    cdeg_ref[...] = jnp.zeros_like(cdeg_ref)
    real_ref[...] = jnp.zeros_like(real_ref)
    imag_ref[...] = jnp.zeros_like(imag_ref)
    ones = jnp.ones((8, piece), jnp.bfloat16)

    def step(e, carry):
        d = f * cols + e
        held[...] = jnp.zeros_like(held)
        for k in range(cap):

            @pl.when(k < count_ref[d])
            def _():
                at = (d * cap + k) * 2
                row_off = lax.rem(list_ref[at], per)
                col_off = lax.rem(list_ref[at + 1], per)
                weight = weight_ref[e, k]
                w = weight.astype(jnp.float32)
                half = angle_ref[e, k].astype(jnp.float32) * 0.5
                square = half * half
                sin_half = half * horner(SIN_TERMS, square)
                cos_half = horner(COS_TERMS, square)
                cos_full = 1.0 - 2.0 * (sin_half * sin_half)
                sin_full = 2.0 * (sin_half * cos_half)
                rows = pl.ds(pl.multiple_of(e * piece + row_off * tile, tile), tile)
                lanes = pl.ds(pl.multiple_of(col_off * tile, tile), tile)
                real_ref[rows, lanes] = (w * cos_full).astype(jnp.bfloat16)
                imag_ref[rows, lanes] = (w * sin_full).astype(jnp.bfloat16)
                held[pl.ds(pl.multiple_of(row_off * tile, tile), tile), lanes] = weight

        block = held[...]
        rdeg_ref[e] += dot(ones, block, NT)
        cdeg_ref[0] += dot(ones, block, NN)
        return carry

    lax.fori_loop(0, cols, step, 0)


def main_kernel(
    rows, cols, images_all, width, real_any, imag_any, rdeg_ref, cdeg_ref, init_ref, out_ref,
    real, imag, rdeg_recv, cdeg_recv, xsend, xrow, xcol, fsend, frecv, msend, mrecv,
    grow_send, grow, gcol_send, gcol, basis, scales,
    load_sem, drs, drr, dcs, dcr, xrs, xrr, xcs, xcr, fs, fr, ms, mr_, grs, grr, gcs, gcr,
):
    a = lax.axis_index("row")
    b = lax.axis_index("col")
    piece = init_ref.shape[1]

    def row_peer(k):
        return lax.rem(a + k, rows)

    def col_peer(k):
        return lax.rem(b + k, cols)

    def row_copy(src, dst, ssem, rsem, k):
        return pltpu.make_async_remote_copy(
            src_ref=src, dst_ref=dst.at[a], send_sem=ssem.at[k], recv_sem=rsem.at[k],
            device_id=(row_peer(k), b), device_id_type=MESH)

    def col_copy(src, dst, ssem, rsem, k):
        return pltpu.make_async_remote_copy(
            src_ref=src, dst_ref=dst.at[b], send_sem=ssem.at[k], recv_sem=rsem.at[k],
            device_id=(a, col_peer(k)), device_id_type=MESH)

    loads = [pltpu.make_async_copy(real_any, real, load_sem.at[0]),
             pltpu.make_async_copy(imag_any, imag, load_sem.at[1])]
    for load in loads:
        load.start()

    barrier = pltpu.get_barrier_semaphore()
    for k in range(1, rows):
        pl.semaphore_signal(barrier, inc=1, device_id=(row_peer(k), b), device_id_type=MESH)
    for k in range(1, cols):
        pl.semaphore_signal(barrier, inc=1, device_id=(a, col_peer(k)), device_id_type=MESH)
    pl.semaphore_wait(barrier, rows + cols - 2)

    copies = [col_copy(rdeg_ref.at[col_peer(k)], rdeg_recv, dcs, dcr, k) for k in range(1, cols)]
    copies += [row_copy(cdeg_ref.at[row_peer(k)], cdeg_recv, drs, drr, k) for k in range(1, rows)]
    for copy in copies:
        copy.start()
    rdeg_recv[b] = rdeg_ref[b]
    cdeg_recv[a] = cdeg_ref[a]
    basis[...] = init_ref[...]
    for copy in copies:
        copy.wait()
    degree = rdeg_recv[0]
    for e in range(1, cols):
        degree = degree + rdeg_recv[e]
    for f in range(rows):
        degree = degree + cdeg_recv[f]
    scales[...] = 1.0 / jnp.sqrt(0.5 * degree)
    for load in loads:
        load.wait()

    def turned(x):
        return jnp.concatenate([-x[width:], x[:width]], 0)

    row_id = lax.broadcasted_iota(jnp.int32, (width, 4 * width), 0)
    lane_id = lax.broadcasted_iota(jnp.int32, (width, 4 * width), 1)

    def iteration(t, carry):
        scale = scales[0:1]
        xs = (basis[...] * scale).astype(jnp.bfloat16)
        xsend[...] = xs
        row_x = [row_copy(xsend, xrow, xrs, xrr, k) for k in range(1, rows)]
        col_x = [col_copy(xsend, xcol, xcs, xcr, k) for k in range(1, cols)]
        for copy in row_x + col_x:
            copy.start()
        xrow[a] = xs
        xcol[b] = xs
        for copy in row_x:
            copy.wait_recv()

        def forward(e):
            total = None
            at = pl.ds(pl.multiple_of(e * piece, piece), piece)
            for f in range(rows):
                x = xrow[f]
                lanes = slice(f * piece, (f + 1) * piece)
                term = dot(x, real[at, lanes], NT) + dot(turned(x), imag[at, lanes], NT)
                total = term if total is None else total + term
            return total.astype(fsend.dtype)

        def forward_step(k, carry):
            fsend[k] = forward(col_peer(k))
            col_copy(fsend.at[k], frecv, fs, fr, k).start()
            return carry

        lax.fori_loop(1, cols, forward_step, 0)
        frecv[b] = forward(b)
        for copy in col_x:
            copy.wait_recv()

        def mirror(f):
            total = None
            lanes = pl.ds(pl.multiple_of(f * piece, piece), piece)
            for e in range(cols):
                x = xcol[e]
                at = slice(e * piece, (e + 1) * piece)
                term = dot(x, real[at, lanes], NN) - dot(turned(x), imag[at, lanes], NN)
                total = term if total is None else total + term
            return total.astype(msend.dtype)

        def mirror_step(k, carry):
            msend[k] = mirror(row_peer(k))
            row_copy(msend.at[k], mrecv, ms, mr_, k).start()
            return carry

        lax.fori_loop(1, rows, mirror_step, 0)
        mrecv[a] = mirror(a)
        for copy in row_x + col_x:
            copy.wait_send()
        for k in range(1, cols):
            col_copy(fsend.at[k], frecv, fs, fr, k).wait()
        for k in range(1, rows):
            row_copy(msend.at[k], mrecv, ms, mr_, k).wait()
        total = frecv[0].astype(jnp.float32)
        for e in range(1, cols):
            total = total + frecv[e].astype(jnp.float32)
        for f in range(rows):
            total = total + mrecv[f].astype(jnp.float32)
        image = total * (0.5 * scale)

        first, second = image[:width], image[width:]
        both = jnp.concatenate([first, second], 1)
        other = jnp.concatenate([second, -first], 1)
        right = jnp.concatenate([both, other, jnp.zeros((2 * width, 2 * piece), jnp.float32)], 0)
        gram = dot(both, right, NT, HIGH)
        upper = width // 2
        packed = gram[:upper] + pltpu.roll(gram[upper:], 2 * width, 1)
        grow_send[...] = packed
        gram_row = [row_copy(grow_send, grow, grs, grr, k) for k in range(1, rows)]
        for copy in gram_row:
            copy.start()
        grow[a] = packed
        for copy in gram_row:
            copy.wait()
        packed = grow[0]
        for f in range(1, rows):
            packed = packed + grow[f]
        gcol_send[...] = packed
        gram_col = [col_copy(gcol_send, gcol, gcs, gcr, k) for k in range(1, cols)]
        for copy in gram_col:
            copy.start()
        gcol[b] = packed
        for copy in gram_col:
            copy.wait()
        packed = gcol[0]
        for e in range(1, cols):
            packed = packed + gcol[e]
        packed = packed / images_all
        gram = jnp.concatenate([packed, pltpu.roll(packed, 2 * width, 1)], 0)
        inside = lane_id < width
        on_diag = lane_id == row_id
        trace = jnp.sum(jnp.where(on_diag, gram, 0.0), axis=(0, 1), keepdims=True)
        ridge = 0.01 * trace / width + 1e-06
        ar = jnp.where(inside, gram, jnp.where(lane_id == row_id + width, 1.0, 0.0))
        ar = ar + jnp.where(on_diag, ridge, 0.0)
        ai = jnp.where(inside, pltpu.roll(gram, 3 * width, 1), 0.0)
        for c in range(width):
            below = row_id[:, 0:1] > c
            inverse = 1.0 / ar[c:c + 1, c:c + 1]
            fac_r = jnp.where(below, ar[:, c:c + 1], 0.0)
            fac_i = jnp.where(below, ai[:, c:c + 1], 0.0)
            top_r = ar[c:c + 1] * inverse
            top_i = ai[c:c + 1] * inverse
            ar = ar - (fac_r * top_r - fac_i * top_i)
            ai = ai - (fac_r * top_i + fac_i * top_r)
        pivots = jnp.sum(jnp.where(on_diag, ar, 0.0), axis=1, keepdims=True)
        roots = 1.0 / jnp.sqrt(pivots)
        ar = ar * roots
        ai = ai * roots
        top = jnp.where(inside, pltpu.roll(ar, 3 * width, 1), ai)
        bottom = jnp.where(inside, -pltpu.roll(ai, 3 * width, 1), ar)
        left = jnp.concatenate([top, bottom], 0)[:, :2 * width]
        basis[...] = dot(left, image, NN, HIGH)
        return carry

    lax.fori_loop(0, ITERS, iteration, 0)
    out_ref[...] = basis[...]


def shards(tile_weight, tile_angle, tile_list, tile_count, init_basis):
    rows = lax.axis_size("row")
    cols = lax.axis_size("col")
    devices = rows * cols
    tile = tile_weight.shape[-1]
    cap = tile_weight.shape[2]
    width = init_basis.shape[1]
    piece = init_basis.shape[2]
    per = piece // tile
    height = cols * piece
    length = rows * piece
    vmem = pltpu.VMEM
    tiles = pl.BlockSpec((cols, cap, tile, tile), lambda f: (f, 0, 0, 0))
    real, imag, rdeg, cdeg = pl.pallas_call(
        functools.partial(prep_kernel, cols, cap, per, tile),
        grid=(rows,),
        in_specs=[pl.BlockSpec(memory_space=pltpu.SMEM)] * 2 + [tiles, tiles],
        out_specs=[
            pl.BlockSpec((height, piece), lambda f: (0, f)),
            pl.BlockSpec((height, piece), lambda f: (0, f)),
            pl.BlockSpec((cols, 8, piece), lambda f: (0, 0, 0)),
            pl.BlockSpec((1, 8, piece), lambda f: (f, 0, 0)),
        ],
        out_shape=[
            jax.ShapeDtypeStruct((height, length), jnp.bfloat16),
            jax.ShapeDtypeStruct((height, length), jnp.bfloat16),
            jax.ShapeDtypeStruct((cols, 8, piece), jnp.float32),
            jax.ShapeDtypeStruct((rows, 8, piece), jnp.float32),
        ],
        scratch_shapes=[vmem((piece, piece), jnp.bfloat16)],
        name="prep",
    )(
        tile_list.reshape(devices * cap * 2),
        tile_count.reshape(devices),
        tile_weight.reshape(devices, cap, tile, tile),
        tile_angle.reshape(devices, cap, tile, tile),
    )
    side = 2 * width
    small = (width // 2, 4 * width)
    f32, bf16 = jnp.float32, jnp.bfloat16
    dma = pltpu.SemaphoreType.DMA
    anywhere = pl.BlockSpec(memory_space=pl.ANY)
    local = pl.BlockSpec(memory_space=pltpu.VMEM)
    out = pl.pallas_call(
        functools.partial(main_kernel, rows, cols, float(piece * devices), width),
        in_specs=[anywhere, anywhere, local, local, local],
        out_specs=local,
        out_shape=jax.ShapeDtypeStruct((side, piece), f32),
        scratch_shapes=[
            vmem((height, length), bf16), vmem((height, length), bf16),
            vmem((cols, 8, piece), f32), vmem((rows, 8, piece), f32),
            vmem((side, piece), bf16), vmem((rows, side, piece), bf16), vmem((cols, side, piece), bf16),
            vmem((cols, side, piece), PART_DTYPE), vmem((cols, side, piece), PART_DTYPE),
            vmem((rows, side, piece), PART_DTYPE), vmem((rows, side, piece), PART_DTYPE),
            vmem(small, f32), vmem((rows,) + small, f32), vmem(small, f32), vmem((cols,) + small, f32),
            vmem((side, piece), f32), vmem((8, piece), f32),
            dma((2,)),
            dma((rows,)), dma((rows,)), dma((cols,)), dma((cols,)),
            dma((rows,)), dma((rows,)), dma((cols,)), dma((cols,)),
            dma((cols,)), dma((cols,)), dma((rows,)), dma((rows,)),
            dma((rows,)), dma((rows,)), dma((cols,)), dma((cols,)),
        ],
        compiler_params=pltpu.CompilerParams(
            collective_id=0, has_side_effects=True, vmem_limit_bytes=60 * 1024 * 1024
        ),
        name="main",
    )(real, imag, rdeg, cdeg, init_basis.reshape(side, piece))
    return out.reshape(2, width, piece)


def solution(mesh):
    placed = (
        P(("row", "col"), None, None, None, None),
        P(("row", "col"), None, None, None, None),
        P(("row", "col"), None, None, None),
        P(("row", "col"), None),
        P(None, None, ("row", "col")),
    )
    return jax.shard_map(
        shards, mesh=mesh, in_specs=placed, out_specs=P(None, None, ("row", "col")), check_vma=False
    )
```

time: 1160 us -> 98.4 us (0.08)
  matrix products: 323 us -> 0 us
  blocking collectives: 224 us -> 0 us
  waiting for transfers between devices: 193 us -> 0 us
  between operations: 142 us -> 0.01 us
  local copies, waits for them, and re-layouts: 139 us -> 2.92 us
  other arithmetic: 124 us -> 0 us
  Pallas kernels: 0 us -> 95.3 us
    dot_general x795 -> x0, matrix products: 323 us -> none  [the longest x775 279 us: highest_dot(): jnp.dot(left, right, precision=lax.Precision.HIGHEST, preferred_element_t...]
    reduce_scatter x3 -> x0, waiting for transfers between devices: 163 us -> none  [shards(): lax.psum_scatter(partial_value.reshape(2, columns, group_rows * tile), 'c...]
    psum x3 -> x0, blocking collectives: 121 us -> none  [shards(): gram_real, gram_imag = lax.psum((gram_real, gram_imag), ('row', 'col'))]
    slice x318 -> x0, local copies, waits for them, and re-layouts: 115 us -> none  [the longest x99 63.6 us: orthonormal(): pivot = jnp.sqrt(gram_real[column, column] - prod_real[column])]
    pallas_call x0 -> x2, Pallas kernels: none -> 95.3 us  [the longest x1 82.9 us: shards(): pl.pallas_call(functools.partial(main_kernel, rows, cols, float(piece * d...]
    another operation x131 -> x0, other arithmetic: 80.5 us -> none
    all_to_all x2 -> x0, blocking collectives: 67.7 us -> none  [the longest x1 53.4 us: shards(): lax.all_to_all(tile_angle.reshape(devices, pair_cap, tile, tile), ('row',...]
    convert_element_type x5 -> x0, other arithmetic: 35.6 us -> none  [the longest x2 35.6 us: complex_tiles(): (weight_f * jnp.cos(angle_f)).astype(jnp.bfloat16)]
  transfers between devices with their start and end apart: 4 -> 0, of which waited for: 4 -> 0; matrix products, arithmetic and copies ran while one was open for 3% -> 0% of each run, Pallas kernels for 0% -> 0%
where the time goes in v1:
time: 98.4 us; the launch traced here: 98.3 us
  Pallas kernels  95.3 us (97%)
  local copies, waits for them, and re-layouts  2.92 us (3%)
    pallas_call x1, Pallas kernels, shards(): pl.pallas_call(functools.partial(main_kernel, rows, cols, float(piece * d...  82.9 us
    pallas_call x1, Pallas kernels, shards(): pl.pallas_call(functools.partial(prep_kernel, cols, cap, per, tile), grid...  12.5 us
    unnamed x2, local copies, waits for them, and re-layouts  2.25 us

profile of v1, /device:TPU:0, one launch (start us, length us, event | category | flops | bytes accessed | tf_op | source)
XLA Modules:
  0.0 98.3 jit_solution(14089508106883711032)
XLA Ops:
  0.0 0.8 copy.7
  0.8 0.7 reshape.18.list_ref
  1.5 12.5 %prep.1 = (bf16[2048,1024]{1,0:T(8,128)(2,1)}, bf16[2048,1024]{1,0:T(8,128)(2,1)}, f32[8,8,256]{2,1,0:T(8,128)}, f32[4,8,256]{2,1,0:T(8,128)}) custom-call(s32[128]{0:T(128)} %reshape.18.list_ref, s32[32]{0:T(128)} %bitcast.9, bf16[32,2,128,128]{3,2,1,0:T(8,128)(2,1)} %bitcast.5, bf16[32,2,128,128]{3,2,1,0:T(8,128)(2,1)} %bitcast.6), custom_call_target="tpu_custom_call" | custom-call | tf_op jit(solution)/shard_map/prep/pallas_call | solution.py:273
  13.9 82.9 %main.1 = f32[64,256]{1,0:T(8,128)} custom-call(bf16[2048,1024]{1,0:T(8,128)(2,1)} %get-tuple-element.9.real_any, bf16[2048,1024]{1,0:T(8,128)(2,1)} %get-tuple-element.10.imag_any, f32[8,8,256]{2,1,0:T(8,128)} %get-tuple-element.11.rdeg_ref, f32[4,8,256]{2,1,0:T(8,128)} %get-tuple-element.12.cdeg_ref, f32[64,256]{1,0:T(8,128)} %bitcast.8), custom_call_target="tpu_custom_call" | custom-call | tf_op jit(solution)/shard_map/main/pallas_call | solution.py:303
  96.8 1.5 %copy.9 = f32[2,32,256]{2,1,0:T(8,128)} copy(f32[2,32,256]{2,1,0:T(8,128)} %bitcast.7) | data formatting | bytes 131072

commit v2 on v1

--- a/solution.py
+++ b/solution.py
@@ -36,14 +36,12 @@
     def _():
         rdeg_ref[...] = jnp.zeros_like(rdeg_ref)
 
-    cdeg_ref[...] = jnp.zeros_like(cdeg_ref)
     real_ref[...] = jnp.zeros_like(real_ref)
     imag_ref[...] = jnp.zeros_like(imag_ref)
-    ones = jnp.ones((8, piece), jnp.bfloat16)
+    held[...] = jnp.zeros_like(held)
 
     def step(e, carry):
         d = f * cols + e
-        held[...] = jnp.zeros_like(held)
         for k in range(cap):
 
             @pl.when(k < count_ref[d])
@@ -63,14 +61,16 @@
                 lanes = pl.ds(pl.multiple_of(col_off * tile, tile), tile)
                 real_ref[rows, lanes] = (w * cos_full).astype(jnp.bfloat16)
                 imag_ref[rows, lanes] = (w * sin_full).astype(jnp.bfloat16)
-                held[pl.ds(pl.multiple_of(row_off * tile, tile), tile), lanes] = weight
-
-        block = held[...]
-        rdeg_ref[e] += dot(ones, block, NT)
-        cdeg_ref[0] += dot(ones, block, NN)
+                held[rows, lanes] = weight
+
         return carry
 
     lax.fori_loop(0, cols, step, 0)
+    across = jnp.ones((8, piece), jnp.bfloat16)
+    down = jnp.ones((8, cols * piece), jnp.bfloat16)
+    cdeg_ref[0] = dot(down, held[...], NN)
+    for e in range(cols):
+        rdeg_ref[e] += dot(across, held[e * piece:(e + 1) * piece], NT)
 
 
 def main_kernel(
@@ -286,7 +286,7 @@
             jax.ShapeDtypeStruct((cols, 8, piece), jnp.float32),
             jax.ShapeDtypeStruct((rows, 8, piece), jnp.float32),
         ],
-        scratch_shapes=[vmem((piece, piece), jnp.bfloat16)],
+        scratch_shapes=[vmem((height, piece), jnp.bfloat16)],
         name="prep",
     )(
         tile_list.reshape(devices * cap * 2),

time: 98.4 us -> 95.4 us (0.970)
  Pallas kernels: 95.3 us -> 91.6 us
    pallas_call x1, Pallas kernels: 12.5 us -> 8.14 us  [shards(): pl.pallas_call(functools.partial(prep_kernel, cols, cap, per, tile), grid...]
where the time goes in v2:
time: 95.4 us; the launch traced here: 94.6 us
  Pallas kernels  91.6 us (96%)
  local copies, waits for them, and re-layouts  2.92 us (3%)
    pallas_call x1, Pallas kernels, shards(): pl.pallas_call(functools.partial(main_kernel, rows, cols, float(piece * d...  83.5 us
    pallas_call x1, Pallas kernels, shards(): pl.pallas_call(functools.partial(prep_kernel, cols, cap, per, tile), grid...  8.14 us
    unnamed x2, local copies, waits for them, and re-layouts  2.25 us

profile of v2, /device:TPU:0, one launch (start us, length us, event | category | flops | bytes accessed | tf_op | source)
XLA Modules:
  0.0 94.6 jit_solution(13040085378274423408)
XLA Ops:
  0.0 0.8 copy.7
  0.8 0.7 reshape.18.list_ref
  1.5 8.1 %prep.1 = (bf16[2048,1024]{1,0:T(8,128)(2,1)}, bf16[2048,1024]{1,0:T(8,128)(2,1)}, f32[8,8,256]{2,1,0:T(8,128)}, f32[4,8,256]{2,1,0:T(8,128)}) custom-call(s32[128]{0:T(128)} %reshape.18.list_ref, s32[32]{0:T(128)} %bitcast.9, bf16[32,2,128,128]{3,2,1,0:T(8,128)(2,1)} %bitcast.5, bf16[32,2,128,128]{3,2,1,0:T(8,128)(2,1)} %bitcast.6), custom_call_target="tpu_custom_call" | custom-call | tf_op jit(solution)/shard_map/prep/pallas_call | solution.py:273
  9.6 83.5 %main.1 = f32[64,256]{1,0:T(8,128)} custom-call(bf16[2048,1024]{1,0:T(8,128)(2,1)} %get-tuple-element.9.real_any, bf16[2048,1024]{1,0:T(8,128)(2,1)} %get-tuple-element.10.imag_any, f32[8,8,256]{2,1,0:T(8,128)} %get-tuple-element.11.rdeg_ref, f32[4,8,256]{2,1,0:T(8,128)} %get-tuple-element.12.cdeg_ref, f32[64,256]{1,0:T(8,128)} %bitcast.8), custom_call_target="tpu_custom_call" | custom-call | tf_op jit(solution)/shard_map/main/pallas_call | solution.py:303
  93.1 1.5 %copy.9 = f32[2,32,256]{2,1,0:T(8,128)} copy(f32[2,32,256]{2,1,0:T(8,128)} %bitcast.7) | data formatting | bytes 131072
